TPU v7x, 256 devices: a whole 4x4x8 slice. The times are simulated.
256 devices in a mesh: tile: 8 (over y, core), plane: 32 (over x, z).
Axes of the slice: x: 4, y: 4, z: 8, core: 2. Of those that a mesh axis runs over, the one named last changes fastest.
Arguments:
- observed: float32 [2, 32, 512, 256], P(None, 'plane', 'tile'), may hold values from 0.5 to 4
- intersection_strip: float32 [2, 32, 256, 256], P(None, 'plane', 'tile'), may hold values from 0.5 to 4
- axial_taps: float32 [2, 41], replicated, may hold values from 0.05 to 1
- lateral_taps: float32 [2, 15], replicated, may hold values from 0.05 to 1
- extents: int32 [8], P('tile'), may hold values from 1 to 32, as said below
- section_skews: int32 [8], P('tile'), may hold values from 0 to 255
Outputs:
- estimate: float32 [2, 32, 512, 256], P(None, 'plane', 'tile')
Inputs may be any that keep to these rules, and one draw needn't show every extreme that they name: `extents`: entry 0 is not used; the largest of the entries 1 to 7 is 32.
All inputs are finite; a program needn't handle non-finite values.
Results may differ from a plain program's by a relative error of at most 0.00005.
Values sent between devices are 32-bit elements; how exact they have to be, the bound alone decides.
A program may use at most 64 MiB of HBM per device.

v0:
```python
import jax
import jax.numpy as jnp
from jax import lax
from jax.sharding import PartitionSpec as P

ITERS = 2
highest = lax.Precision.HIGHEST


def with_halo(block, sides, width):
    for axis, dim in sides:
        count = lax.axis_size(axis)
        forward = [(i, i + 1) for i in range(count - 1)]
        backward = [(target, source) for source, target in forward]
        low = lax.ppermute(
            lax.slice_in_dim(block, block.shape[dim] - width, None, axis=dim), axis, forward
        )
        high = lax.ppermute(lax.slice_in_dim(block, 0, width, axis=dim), axis, backward)
        block = jnp.concatenate([low, block, high], axis=dim)
    return block


def from_behind(array, axis, by):
    length = lax.axis_size(axis)
    pairs = [(i, i + by) for i in range(length) if 0 <= i + by < length]
    return lax.ppermute(array, axis, pairs)


def band_matrix(kernel, row_count, col_count, offset):
    offsets = (
        jnp.arange(col_count, dtype=jnp.int32)[None, :]
        - jnp.arange(row_count, dtype=jnp.int32)[:, None]
        + offset
    )
    tap_ids = jnp.arange(kernel.shape[1], dtype=jnp.int32)
    one_hot = jnp.where(offsets[:, :, None] == tap_ids[None, None, :], 1.0, 0.0).astype(jnp.float32)
    return jnp.einsum("ck,rsk->crs", kernel, one_hot, precision=highest)


def blur_rows_x(volume, x_band):
    chans, planes, rowsn, voxels = volume.shape
    blocks = volume.reshape(chans, planes, rowsn, voxels // 128, 128)
    padded = jnp.pad(blocks, ((0, 0), (0, 0), (0, 0), (1, 1), (0, 0)))
    window = jnp.concatenate(
        [padded[:, :, :, :-2], padded[:, :, :, 1:-1], padded[:, :, :, 2:]], axis=4
    )
    result = jnp.einsum("czynw,cow->czyno", window, x_band, precision=highest)
    return result.reshape(chans, planes, rowsn, voxels)


def blur_rows_y(volume, y_band, half_width):
    padded = with_halo(volume, (("tile", 2),), half_width)
    return jnp.einsum("cyp,czpx->czyx", y_band, padded, precision=highest)


def axial_pass(pencils, z_band):
    return jnp.einsum("cij,cjw->ciw", z_band, pencils, precision=highest)


def to_pencils(volume):
    chans, planes, rowsn, voxels = volume.shape
    return lax.all_to_all(
        volume.reshape(chans, planes, rowsn * voxels),
        "plane",
        split_axis=2,
        concat_axis=1,
        tiled=True,
    )


def to_planes(pencils, row_count, col_count):
    flattened = lax.all_to_all(pencils, "plane", split_axis=1, concat_axis=2, tiled=True)
    return flattened.reshape(flattened.shape[0], flattened.shape[1], row_count, col_count)


def shards(observed, intersection_strip, axial_taps, lateral_taps, extents, section_skews):
    chans, planes, row_count, col_count = observed.shape
    strip_count = intersection_strip.shape[2]
    received = from_behind(intersection_strip, "tile", 1)
    turned = jnp.roll(received, section_skews[0], axis=3)
    reach_rows = jnp.where(lax.axis_index("tile") == 0, 0, extents[0])
    inside = (jnp.arange(strip_count, dtype=jnp.int32) < reach_rows)[None, None, :, None]
    top_rows = observed[:, :, :strip_count]
    joined_obs = jnp.concatenate(
        [jnp.where(inside, 0.5 * (top_rows + turned), top_rows), observed[:, :, strip_count:]],
        axis=2,
    )
    axial_width = axial_taps.shape[1]
    lateral_width = lateral_taps.shape[1]
    axial_half = axial_width // 2
    lateral_half = lateral_width // 2
    total_planes = planes * lax.axis_size("plane")
    axial_flip = jnp.flip(axial_taps, axis=1)
    lateral_flip = jnp.flip(lateral_taps, axis=1)
    z_forward = band_matrix(axial_taps, total_planes, total_planes, axial_half)
    z_adjoint = band_matrix(axial_flip, total_planes, total_planes, axial_half)
    y_forward = band_matrix(lateral_taps, row_count, row_count + 2 * lateral_half, 0)
    y_adjoint = band_matrix(lateral_flip, row_count, row_count + 2 * lateral_half, 0)
    x_forward = band_matrix(lateral_taps, 128, 384, lateral_half - 128)
    x_adjoint = band_matrix(lateral_flip, 128, 384, lateral_half - 128)
    estimate = joined_obs
    for sweep in range(ITERS):
        lateral_done = blur_rows_y(blur_rows_x(estimate, x_forward), y_forward, lateral_half)
        blurred = to_planes(axial_pass(to_pencils(lateral_done), z_forward), row_count, col_count)
        quotient = joined_obs / blurred
        spread_back = to_planes(axial_pass(to_pencils(quotient), z_adjoint), row_count, col_count)
        estimate = estimate * blur_rows_x(
            blur_rows_y(spread_back, y_adjoint, lateral_half), x_adjoint
        )
    return estimate


def solution(mesh):
    in_specs = (
        P(None, "plane", "tile", None),
        P(None, "plane", "tile", None),
        P(),
        P(),
        P("tile"),
        P("tile"),
    )
    out_specs = P(None, "plane", "tile", None)
    return jax.shard_map(shards, mesh=mesh, in_specs=in_specs, out_specs=out_specs, check_vma=False)
```

profile of v0, /device:TPU:1, one launch (start us, length us, event | category | flops | bytes accessed | tf_op | source)
XLA Modules:
  0.0 619.2 jit_solution(13503194051513561913)
XLA Ops:
  0.0 4.6 collective-permute-start
  6.0 3.3 fusion.10
  11.3 1.9 collective-permute-start.1
  13.3 2.4 collective-permute-start.2
  16.9 1.4 collective-permute-done.2
  18.6 4.6 copy.141
  23.8 74.4 %reduce = f32[16384,2]{1,0:T(8,128)} reduce(f32[16384,1,2]{2,1,0:T(1,128)} %bitcast.131, f32[]{:T(128)} %broadcast.47), dimensions={1}, to_apply=%bitcast.113.reduce_sub_computation | reduce | bytes 262148
  98.2 8.2 %reshape.294 = f32[32,1,1024]{2,1,0:T(1,128)} reshape(f32[16384,2]{1,0:T(8,128)} %reduce) | data formatting | bytes 262144
  106.4 11.2 %all-to-all-start = ((f32[32,1,1024]{2,1,0:T(1,128)}), f32[32,1,1024]{2,1,0:T(1,128)S(1)}, u32[]{:S(2)}, u32[]{:S(2)}) async-start(f32[32,1,1024]{2,1,0:T(1,128)} %reshape.294), calls=%async_computation | async-start | bytes 262144 | tf_op jit(solution)/shard_map/all_to_all | solution.py:62
  117.7 2.2 convolution_bitcast_fusion.6
  119.9 7.5 %all-to-all-done = f32[32,1,1024]{2,1,0:T(1,128)S(1)} async-done(((f32[32,1,1024]{2,1,0:T(1,128)}), f32[32,1,1024]{2,1,0:T(1,128)S(1)}, u32[]{:S(2)}, u32[]{:S(2)}) %all-to-all-start) | async-done | bytes 131104 | tf_op jit(solution)/shard_map/all_to_all | solution.py:62
  128.3 14.9 %reshape.295 = f32[16384,1,2]{2,1,0:T(1,128)} reshape(f32[32,1024]{1,0:T(8,128)S(1)} %reduce.1) | data formatting | bytes 262144
  143.2 5.2 copy.142
  149.5 3.9 all-to-all-start.1
  153.5 9.1 %all-to-all-done.1 = f32[2,32,512]{2,0,1:T(2,128)S(1)} async-done(((f32[2,32,512]{2,0,1:T(2,128)}), f32[2,32,512]{2,0,1:T(2,128)S(1)}, u32[]{:S(2)}, u32[]{:S(2)}) %all-to-all-start.1) | async-done | bytes 131104 | tf_op jit(solution)/shard_map/all_to_all | solution.py:72
  162.6 12.1 %copy.105 = f32[2,1,16384]{0,1,2:T(1,128)} copy(f32[2,1,16384]{2,0,1:T(2,128)S(1)} %div.24) | data formatting | bytes 262144 | tf_op jit(solution)/shard_map/div | solution.py:105
  174.7 74.4 %reduce.2 = f32[16384,2]{1,0:T(8,128)} reduce(f32[16384,1,2]{2,1,0:T(1,128)} %bitcast.132, f32[]{:T(128)} %broadcast.47), dimensions={1}, to_apply=%bitcast.115.reduce_sub_computation | reduce | bytes 262148
  249.1 8.2 %reshape.296 = f32[32,1,1024]{2,1,0:T(1,128)} reshape(f32[16384,2]{1,0:T(8,128)} %reduce.2) | data formatting | bytes 262144
  257.4 4.8 all-to-all-start.2
  262.2 2.2 convolution_bitcast_fusion.7
  264.4 6.9 %all-to-all-done.2 = f32[32,1,1024]{2,1,0:T(1,128)S(1)} async-done(((f32[32,1,1024]{2,1,0:T(1,128)}), f32[32,1,1024]{2,1,0:T(1,128)S(1)}, u32[]{:S(2)}, u32[]{:S(2)}) %all-to-all-start.2) | async-done | bytes 131104 | tf_op jit(solution)/shard_map/all_to_all | solution.py:62
  272.2 14.9 %reshape.297 = f32[16384,1,2]{2,1,0:T(1,128)} reshape(f32[32,1024]{1,0:T(8,128)S(1)} %reduce.3) | data formatting | bytes 262144
  287.1 5.2 copy.143
  293.4 3.9 all-to-all-start.3
  297.8 8.5 %all-to-all-done.3 = f32[2,32,512]{2,0,1:T(2,128)S(1)} async-done(((f32[2,32,512]{2,0,1:T(2,128)}), f32[2,32,512]{2,0,1:T(2,128)S(1)}, u32[]{:S(2)}, u32[]{:S(2)}) %all-to-all-start.3) | async-done | bytes 131104 | tf_op jit(solution)/shard_map/all_to_all | solution.py:72
  306.4 7.1 %collective-permute-start.3 = (f32[2,1,7,256]{3,2,0,1:T(8,128)S(1)}, f32[2,1,7,256]{3,2,0,1:T(8,128)S(1)}, u32[]{:S(2)}, u32[]{:S(2)}) collective-permute-start(f32[2,1,7,256]{3,2,0,1:T(8,128)S(1)} %get-tuple-element.15), channel_id=1, source_target_pairs={{0,32},{32,64},{64,96},{96,128},{128,160},{160,192},{192,224},{1,3... | collective-permute-start | bytes 43016 | tf_op jit(solution)/shard_map/ppermute | solution.py:15
  313.6 1.9 collective-permute-start.4
  315.5 2.6 fusion.13
  320.6 3.3 collective-permute-start.5
  323.9 2.3 collective-permute-start.6
  326.2 2.7 collective-permute-done.6
  329.2 4.6 copy.148
  333.8 74.4 %reduce.4 = f32[16384,2]{1,0:T(8,128)} reduce(f32[16384,1,2]{2,1,0:T(1,128)} %bitcast.133, f32[]{:T(128)} %broadcast.47), dimensions={1}, to_apply=%bitcast.117.reduce_sub_computation | reduce | bytes 262148
  408.3 7.6 %reshape.298 = f32[32,1,1024]{2,1,0:T(1,128)S(1)} reshape(f32[16384,2]{1,0:T(8,128)} %reduce.4) | data formatting | bytes 262144
  415.9 12.5 %all_to_all.84 = f32[32,1,1024]{2,1,0:T(1,128)S(1)} all-to-all(f32[32,1,1024]{2,1,0:T(1,128)S(1)} %reshape.298), channel_id=1, replica_groups=mesh['tile'=8,'plane'=32] {'plane'}, dimensions={0} | all-to-all | bytes 262144 | tf_op jit(solution)/shard_map/all_to_all | solution.py:62
  429.3 14.9 %reshape.299 = f32[16384,1,2]{2,1,0:T(1,128)} reshape(f32[32,1024]{1,0:T(8,128)S(1)} %reduce.5) | data formatting | bytes 262144
  444.2 5.2 copy.149
  449.8 12.7 %all_to_all.85 = f32[2,32,512]{2,0,1:T(2,128)S(1)} all-to-all(f32[2,32,512]{2,0,1:T(2,128)S(1)} %copy.123), channel_id=1, replica_groups=mesh['tile'=8,'plane'=32] {'plane'}, dimensions={1} | all-to-all | bytes 262144 | tf_op jit(solution)/shard_map/all_to_all | solution.py:72
  462.5 12.1 %copy.124 = f32[2,1,16384]{0,1,2:T(1,128)} copy(f32[2,1,16384]{2,0,1:T(2,128)S(1)} %div.25) | data formatting | bytes 262144 | tf_op jit(solution)/shard_map/div | solution.py:105
  474.6 74.4 %reduce.6 = f32[16384,2]{1,0:T(8,128)} reduce(f32[16384,1,2]{2,1,0:T(1,128)} %bitcast.134, f32[]{:T(128)} %broadcast.47), dimensions={1}, to_apply=%bitcast.119.reduce_sub_computation | reduce | bytes 262148
  549.1 7.6 %reshape.300 = f32[32,1,1024]{2,1,0:T(1,128)S(1)} reshape(f32[16384,2]{1,0:T(8,128)} %reduce.6) | data formatting | bytes 262144
  556.7 13.6 %all_to_all.86 = f32[32,1,1024]{2,1,0:T(1,128)S(1)} all-to-all(f32[32,1,1024]{2,1,0:T(1,128)S(1)} %reshape.300), channel_id=1, replica_groups=mesh['tile'=8,'plane'=32] {'plane'}, dimensions={0} | all-to-all | bytes 262144 | tf_op jit(solution)/shard_map/all_to_all | solution.py:62
  571.2 14.9 %reshape.301 = f32[16384,1,2]{2,1,0:T(1,128)} reshape(f32[32,1024]{1,0:T(8,128)S(1)} %reduce.7) | data formatting | bytes 262144
  586.1 5.2 copy.150
  591.7 12.7 %all_to_all.87 = f32[2,32,512]{2,0,1:T(2,128)S(1)} all-to-all(f32[2,32,512]{2,0,1:T(2,128)S(1)} %copy.127), channel_id=1, replica_groups=mesh['tile'=8,'plane'=32] {'plane'}, dimensions={1} | all-to-all | bytes 262144 | tf_op jit(solution)/shard_map/all_to_all | solution.py:72
  604.5 7.6 %collective-permute-start.7 = (f32[2,1,7,256]{3,2,0,1:T(8,128)S(1)}, f32[2,1,7,256]{3,2,0,1:T(8,128)S(1)}, u32[]{:S(2)}, u32[]{:S(2)}) collective-permute-start(f32[2,1,7,256]{3,2,0,1:T(8,128)S(1)} %get-tuple-element.7), channel_id=1, source_target_pairs={{0,32},{32,64},{64,96},{96,128},{128,160},{160,192},{192,224},{1,3... | collective-permute-start | bytes 43016 | tf_op jit(solution)/shard_map/ppermute | solution.py:15
  612.1 1.9 collective-permute-start.8
  614.2 2.9 collective-permute-done.8
  (74 shorter events, 16.2 us)
Async XLA Ops:
  0.0 9.3 %collective-permute-start = (f32[2,1,32,256]{3,2,0,1:T(8,128)}, f32[2,1,32,256]{3,2,0,1:T(8,128)S(1)}, u32[]{:S(2)}, u32[]{:S(2)}) collective-permute-start(f32[2,1,32,256]{3,2,0,1:T(8,128)} %bitcast.146), channel_id=1, source_target_pairs={{0,32},{32,64},{64,96},{96,128},{128,160},{160,192},{192,224},{1,3... | collective-permute-start | bytes 196616 | tf_op jit(solution)/shard_map/ppermute | solution.py:26
  11.3 5.5 collective-permute-start.1
  13.3 5.1 collective-permute-start.2
  98.2 19.5 %copy-start = (f32[2,41]{1,0:T(2,128)S(1)}, f32[2,41]{1,0:T(2,128)}, u32[]{:S(2)}) copy-start(f32[2,41]{1,0:T(2,128)} %param.8) | copy-start | bytes 988
  106.4 21.0 %all-to-all-start = ((f32[32,1,1024]{2,1,0:T(1,128)}), f32[32,1,1024]{2,1,0:T(1,128)S(1)}, u32[]{:S(2)}, u32[]{:S(2)}) async-start(f32[32,1,1024]{2,1,0:T(1,128)} %reshape.294), calls=%async_computation | async-start | bytes 262144 | tf_op jit(solution)/shard_map/all_to_all | solution.py:62
  149.5 13.0 %all-to-all-start.1 = ((f32[2,32,512]{2,0,1:T(2,128)}), f32[2,32,512]{2,0,1:T(2,128)S(1)}, u32[]{:S(2)}, u32[]{:S(2)}) async-start(f32[2,32,512]{2,0,1:T(2,128)} %copy.104), calls=%async_computation.1 | async-start | bytes 262144 | tf_op jit(solution)/shard_map/all_to_all | solution.py:72
  257.4 13.9 %all-to-all-start.2 = ((f32[32,1,1024]{2,1,0:T(1,128)}), f32[32,1,1024]{2,1,0:T(1,128)S(1)}, u32[]{:S(2)}, u32[]{:S(2)}) async-start(f32[32,1,1024]{2,1,0:T(1,128)} %reshape.296), calls=%async_computation.2 | async-start | bytes 262144 | tf_op jit(solution)/shard_map/all_to_all | solution.py:62
  272.2 25.0 %copy-start.1 = (f32[2,15]{1,0:T(2,128)S(1)}, f32[2,15]{1,0:T(2,128)}, u32[]{:S(2)}) copy-start(f32[2,15]{1,0:T(2,128)} %param.9) | copy-start | bytes 364
  293.4 13.0 %all-to-all-start.3 = ((f32[2,32,512]{2,0,1:T(2,128)}), f32[2,32,512]{2,0,1:T(2,128)S(1)}, u32[]{:S(2)}, u32[]{:S(2)}) async-start(f32[2,32,512]{2,0,1:T(2,128)} %copy.108), calls=%async_computation.3 | async-start | bytes 262144 | tf_op jit(solution)/shard_map/all_to_all | solution.py:72
  306.4 11.8 %collective-permute-start.3 = (f32[2,1,7,256]{3,2,0,1:T(8,128)S(1)}, f32[2,1,7,256]{3,2,0,1:T(8,128)S(1)}, u32[]{:S(2)}, u32[]{:S(2)}) collective-permute-start(f32[2,1,7,256]{3,2,0,1:T(8,128)S(1)} %get-tuple-element.15), channel_id=1, source_target_pairs={{0,32},{32,64},{64,96},{96,128},{128,160},{160,192},{192,224},{1,3... | collective-permute-start | bytes 43016 | tf_op jit(solution)/shard_map/ppermute | solution.py:15
  313.6 5.1 collective-permute-start.4
  320.6 5.6 collective-permute-start.5
  323.9 5.1 collective-permute-start.6
  604.5 9.8 %collective-permute-start.7 = (f32[2,1,7,256]{3,2,0,1:T(8,128)S(1)}, f32[2,1,7,256]{3,2,0,1:T(8,128)S(1)}, u32[]{:S(2)}, u32[]{:S(2)}) collective-permute-start(f32[2,1,7,256]{3,2,0,1:T(8,128)S(1)} %get-tuple-element.7), channel_id=1, source_target_pairs={{0,32},{32,64},{64,96},{96,128},{128,160},{160,192},{192,224},{1,3... | collective-permute-start | bytes 43016 | tf_op jit(solution)/shard_map/ppermute | solution.py:15
  612.1 5.1 collective-permute-start.8
where the time goes:
time: 628 us; the launch traced here: 619 us
  other arithmetic  303 us (48%)
  local copies, waits for them, and re-layouts  149 us (24%)
  starting transfers between devices  56.8 us (9%)
  blocking collectives  51.5 us (8%)
  waiting for transfers between devices  39.4 us (6%)
  matrix products  16.8 us (3%)
    unnamed x4, other arithmetic  298 us
    unnamed x13, local copies, waits for them, and re-layouts  91.8 us
    all_to_all x2, blocking collectives, to_pencils(): lax.all_to_all(volume.reshape(chans, planes, rowsn * voxels), 'plane', sp...  26.1 us
    all_to_all x2, blocking collectives, to_planes(): lax.all_to_all(pencils, 'plane', split_axis=1, concat_axis=2, tiled=True)  25.4 us
    div x2, local copies, waits for them, and re-layouts, shards(): quotient = joined_obs / blurred  24.2 us
    all_to_all x4, local copies, waits for them, and re-layouts, to_pencils(): lax.all_to_all(volume.reshape(chans, planes, rowsn * voxels), 'plane', sp...  20.8 us
    ppermute x4, starting transfers between devices, with_halo(): lax.ppermute(lax.slice_in_dim(block, block.shape[dim] - width, None, axis...  19.9 us
    all_to_all x2, waiting for transfers between devices, to_planes(): lax.all_to_all(pencils, 'plane', split_axis=1, concat_axis=2, tiled=True)  17.6 us
  transfers between devices with their start and end apart: 13, of which 8 were waited for; matrix products, arithmetic and copies ran while one was open for 2% of the time, Pallas kernels for 0%

commit v1 on v0

--- a/solution.py
+++ b/solution.py
@@ -59,13 +59,13 @@
 
 def to_pencils(volume):
     chans, planes, rowsn, voxels = volume.shape
-    return lax.all_to_all(
-        volume.reshape(chans, planes, rowsn * voxels),
-        "plane",
-        split_axis=2,
-        concat_axis=1,
-        tiled=True,
+    meet_numbers = lambda view, dim_i, in_dim: jnp.concatenate(
+        lax.all_to_all(
+            jnp.stack(jnp.split(view, lax.axis_size("plane"), axis=dim_i), axis=0), "plane", 0, 0
+        ),
+        axis=in_dim,
     )
+    return meet_numbers(volume.reshape(chans, planes, rowsn * voxels), 2, in_dim=1)
 
 
 def to_planes(pencils, row_count, col_count):

time: 628 us -> 210 us (0.33); the launches traced: 619 us -> 209 us
  other arithmetic: 303 us -> 1.03 us
  local copies, waits for them, and re-layouts: 149 us -> 41.9 us
    unnamed x4 -> x0, other arithmetic: 298 us -> none
    unnamed x13 -> x130, local copies, waits for them, and re-layouts: 91.8 us -> 37.3 us
    div x2 -> x0, local copies, waits for them, and re-layouts: 24.2 us -> none  [shards(): quotient = joined_obs / blurred]
    all_to_all x4 -> x0, local copies, waits for them, and re-layouts: 20.8 us -> none  [to_pencils(): lax.all_to_all(volume.reshape(chans, planes, rowsn * voxels), 'plane', sp...]
    reshape x2, local copies, waits for them, and re-layouts: 9.22 us -> 0.17 us  [to_pencils(): volume.reshape(chans, planes, rowsn * voxels)]
  transfers between devices with their start and end apart: 13 -> 13, of which waited for: 8 -> 8; matrix products, arithmetic and copies ran while one was open for 2% -> 6% of each run, Pallas kernels for 0% -> 0%
where the time goes in v1:
time: 210 us; the launch traced here: 209 us
  starting transfers between devices  56.4 us (27%)
  blocking collectives  51.3 us (24%)
  local copies, waits for them, and re-layouts  41.9 us (20%)
  waiting for transfers between devices  40.4 us (19%)
  matrix products  16.1 us (8%)
  between operations  2.18 us (1%)
    unnamed x130, local copies, waits for them, and re-layouts  37.3 us
    all_to_all x2, blocking collectives, to_pencils(): lax.all_to_all(jnp.stack(jnp.split(view, lax.axis_size('plane'), axis=dim...  26.1 us
    all_to_all x2, blocking collectives, to_planes(): lax.all_to_all(pencils, 'plane', split_axis=1, concat_axis=2, tiled=True)  25.3 us
    ppermute x4, starting transfers between devices, with_halo(): lax.ppermute(lax.slice_in_dim(block, block.shape[dim] - width, None, axis...  20.1 us
    all_to_all x2, waiting for transfers between devices, to_planes(): lax.all_to_all(pencils, 'plane', split_axis=1, concat_axis=2, tiled=True)  17.6 us
    all_to_all x2, starting transfers between devices, to_pencils(): lax.all_to_all(jnp.stack(jnp.split(view, lax.axis_size('plane'), axis=dim...  15.6 us
    all_to_all x2, waiting for transfers between devices, to_pencils(): lax.all_to_all(jnp.stack(jnp.split(view, lax.axis_size('plane'), axis=dim...  14.4 us
    dot_general x6, matrix products, band_matrix(): return jnp.einsum('ck,rsk->crs', kernel, one_hot, precision=highest)  11.4 us
  transfers between devices with their start and end apart: 13, of which 8 were waited for; matrix products, arithmetic and copies ran while one was open for 6% of the time, Pallas kernels for 0%

profile of v1, /device:TPU:1, one launch (start us, length us, event | category | flops | bytes accessed | tf_op | source)
XLA Modules:
  0.0 209.3 jit_solution(3307490047827642545)
XLA Ops:
  0.0 4.6 %collective-permute-start = (f32[2,1,32,256]{3,2,0,1:T(8,128)}, f32[2,1,32,256]{3,2,0,1:T(8,128)S(1)}, u32[]{:S(2)}, u32[]{:S(2)}) collective-permute-start(f32[2,1,32,256]{3,2,0,1:T(8,128)} %bitcast.660), channel_id=1, source_target_pairs={{0,32},{32,64},{64,96},{96,128},{128,160},{160,192},{192,224},{1,3... | collective-permute-start | bytes 196616 | tf_op jit(solution)/shard_map/ppermute | solution.py:26
  6.0 3.4 %fusion.10 = f32[2,128,384,1]{2,0,1,3:T(2,128)S(1)} fusion(s32[128,384]{1,0:T(8,128)S(1)} %subtract_add_fusion, f32[2,15]{1,0:T(2,128)} %param.9), kind=kOutput, calls=%fused_computation.11 | convolution fusion | flops 19169280 | bytes 589944 | tf_op jit(solution)/shard_map/ck,rsk->crs/dot_general | solution.py:37
  9.6 0.6 fusion.20
  10.5 1.9 collective-permute-start.1
  12.5 2.4 %collective-permute-start.2 = (f32[2,1,7,256]{3,2,0,1:T(8,128)S(1)}, f32[2,1,7,256]{3,2,0,1:T(8,128)S(1)}, u32[]{:S(2)}, u32[]{:S(2)}) collective-permute-start(f32[2,1,7,256]{3,2,0,1:T(8,128)S(1)} %get-tuple-element.18), channel_id=1, source_target_pairs={{32,0},{64,32},{96,64},{128,96},{160,128},{192,160},{224,192},{33,... | collective-permute-start | bytes 43016 | tf_op jit(solution)/shard_map/ppermute | solution.py:18
  15.4 2.1 %collective-permute-done.2 = f32[2,1,7,256]{3,2,0,1:T(8,128)S(1)} collective-permute-done((f32[2,1,7,256]{3,2,0,1:T(8,128)S(1)}, f32[2,1,7,256]{3,2,0,1:T(8,128)S(1)}, u32[]{:S(2)}, u32[]{:S(2)}) %collective-permute-start.2) | collective-permute-done | bytes 14368 | tf_op jit(solution)/shard_map/ppermute | solution.py:18
  17.9 0.6 constant_dynamic-update-slice_fusion.31
  18.5 0.6 constant_dynamic-update-slice_fusion.30
  19.7 0.6 constant_dynamic-update-slice_fusion.28
  20.3 0.6 constant_dynamic-update-slice_fusion.27
  20.9 0.6 constant_dynamic-update-slice_fusion.26
  21.5 0.6 constant_dynamic-update-slice_fusion.25
  22.1 0.6 constant_dynamic-update-slice_fusion.24
  22.7 0.6 constant_dynamic-update-slice_fusion.23
  23.3 0.6 constant_dynamic-update-slice_fusion.22
  23.9 0.6 constant_dynamic-update-slice_fusion.21
  24.5 0.6 constant_dynamic-update-slice_fusion.20
  25.0 0.6 constant_dynamic-update-slice_fusion.19
  36.9 11.0 %all-to-all-start = ((f32[32,2,1,512]{3,1,2,0:T(2,128)}), f32[32,2,1,512]{3,1,2,0:T(2,128)S(1)}, u32[]{:S(2)}, u32[]{:S(2)}) async-start(f32[32,2,1,512]{3,1,2,0:T(2,128)} %constant_dynamic-update-slice_fusion), calls=%async_computation | async-start | bytes 262144 | tf_op jit(solution)/shard_map/all_to_all | solution.py:63
  48.0 2.2 %convolution_bitcast_fusion.6 = f32[2,32,32]{2,0,1:T(2,128)S(1)} fusion(s32[32,32]{1,0:T(8,128)S(1)} %subtract_add_fusion.1, f32[2,41]{1,0:T(2,128)S(1)} %copy-done.1), kind=kOutput, calls=%fused_computation.19 | convolution fusion | flops 1091584 | bytes 12616 | tf_op jit(solution)/shard_map/ck,rsk->crs/dot_general | solution.py:37
  50.2 7.6 %all-to-all-done = f32[32,2,1,512]{3,1,2,0:T(2,128)S(1)} async-done(((f32[32,2,1,512]{3,1,2,0:T(2,128)}), f32[32,2,1,512]{3,1,2,0:T(2,128)S(1)}, u32[]{:S(2)}, u32[]{:S(2)}) %all-to-all-start) | async-done | bytes 131104 | tf_op jit(solution)/shard_map/all_to_all | solution.py:63
  58.0 0.8 copy.326
  58.8 3.9 %all-to-all-start.1 = ((f32[2,32,512]{2,0,1:T(2,128)}), f32[2,32,512]{2,0,1:T(2,128)S(1)}, u32[]{:S(2)}, u32[]{:S(2)}) async-start(f32[2,32,512]{2,0,1:T(2,128)} %copy.326), calls=%async_computation.1 | async-start | bytes 262144 | tf_op jit(solution)/shard_map/all_to_all | solution.py:72
  62.7 9.0 %all-to-all-done.1 = f32[2,32,512]{2,0,1:T(2,128)S(1)} async-done(((f32[2,32,512]{2,0,1:T(2,128)}), f32[2,32,512]{2,0,1:T(2,128)S(1)}, u32[]{:S(2)}, u32[]{:S(2)}) %all-to-all-start.1) | async-done | bytes 131104 | tf_op jit(solution)/shard_map/all_to_all | solution.py:72
  71.9 0.6 constant_dynamic-update-slice_fusion.63
  90.9 4.5 %all-to-all-start.2 = ((f32[32,2,1,512]{3,1,2,0:T(2,128)}), f32[32,2,1,512]{3,1,2,0:T(2,128)S(1)}, u32[]{:S(2)}, u32[]{:S(2)}) async-start(f32[32,2,1,512]{3,1,2,0:T(2,128)} %constant_dynamic-update-slice_fusion.32), calls=%async_computation.2 | async-start | bytes 262144 | tf_op jit(solution)/shard_map/all_to_all | solution.py:63
  95.5 2.2 %convolution_bitcast_fusion.7 = f32[2,32,32]{2,0,1:T(2,128)S(1)} fusion(s32[32,32]{1,0:T(8,128)S(1)} %subtract_add_fusion.1, f32[2,41]{1,0:T(2,128)S(1)} %rev.8), kind=kOutput, calls=%fused_computation.20 | convolution fusion | flops 1091584 | bytes 12616 | tf_op jit(solution)/shard_map/ck,rsk->crs/dot_general | solution.py:37
  97.7 6.9 %all-to-all-done.2 = f32[32,2,1,512]{3,1,2,0:T(2,128)S(1)} async-done(((f32[32,2,1,512]{3,1,2,0:T(2,128)}), f32[32,2,1,512]{3,1,2,0:T(2,128)S(1)}, u32[]{:S(2)}, u32[]{:S(2)}) %all-to-all-start.2) | async-done | bytes 131104 | tf_op jit(solution)/shard_map/all_to_all | solution.py:63
  104.9 0.8 copy.329
  105.6 3.9 %all-to-all-start.3 = ((f32[2,32,512]{2,0,1:T(2,128)}), f32[2,32,512]{2,0,1:T(2,128)S(1)}, u32[]{:S(2)}, u32[]{:S(2)}) async-start(f32[2,32,512]{2,0,1:T(2,128)} %copy.329), calls=%async_computation.3 | async-start | bytes 262144 | tf_op jit(solution)/shard_map/all_to_all | solution.py:72
  110.1 8.5 %all-to-all-done.3 = f32[2,32,512]{2,0,1:T(2,128)S(1)} async-done(((f32[2,32,512]{2,0,1:T(2,128)}), f32[2,32,512]{2,0,1:T(2,128)S(1)}, u32[]{:S(2)}, u32[]{:S(2)}) %all-to-all-start.3) | async-done | bytes 131104 | tf_op jit(solution)/shard_map/all_to_all | solution.py:72
  118.7 7.2 %collective-permute-start.3 = (f32[2,1,7,256]{3,2,0,1:T(8,128)S(1)}, f32[2,1,7,256]{3,2,0,1:T(8,128)S(1)}, u32[]{:S(2)}, u32[]{:S(2)}) collective-permute-start(f32[2,1,7,256]{3,2,0,1:T(8,128)S(1)} %get-tuple-element.15), channel_id=1, source_target_pairs={{0,32},{32,64},{64,96},{96,128},{128,160},{160,192},{192,224},{1,3... | collective-permute-start | bytes 43016 | tf_op jit(solution)/shard_map/ppermute | solution.py:15
  125.9 2.1 %collective-permute-start.4 = (f32[2,1,7,256]{3,2,0,1:T(8,128)S(1)}, f32[2,1,7,256]{3,2,0,1:T(8,128)S(1)}, u32[]{:S(2)}, u32[]{:S(2)}) collective-permute-start(f32[2,1,7,256]{3,2,0,1:T(8,128)S(1)} %get-tuple-element.16), channel_id=1, source_target_pairs={{32,0},{64,32},{96,64},{128,96},{160,128},{192,160},{224,192},{33,... | collective-permute-start | bytes 43016 | tf_op jit(solution)/shard_map/ppermute | solution.py:18
  128.0 2.6 %fusion.13 = f32[2,128,384,1]{2,0,1,3:T(2,128)S(1)} fusion(s32[128,384]{1,0:T(8,128)S(1)} %subtract_add_fusion, f32[2,15]{1,0:T(2,128)S(1)} %rev.9), kind=kOutput, calls=%fused_computation.12 | convolution fusion | flops 19169280 | bytes 589944 | tf_op jit(solution)/shard_map/ck,rsk->crs/dot_general | solution.py:37
  131.3 0.6 fusion.25
  132.0 0.6 fusion.30
  132.9 3.4 %collective-permute-start.5 = (f32[2,1,7,256]{3,2,0,1:T(8,128)S(1)}, f32[2,1,7,256]{3,2,0,1:T(8,128)S(1)}, u32[]{:S(2)}, u32[]{:S(2)}) collective-permute-start(f32[2,1,7,256]{3,2,0,1:T(8,128)S(1)} %get-tuple-element.9), channel_id=1, source_target_pairs={{0,32},{32,64},{64,96},{96,128},{128,160},{160,192},{192,224},{1,3... | collective-permute-start | bytes 43016 | tf_op jit(solution)/shard_map/ppermute | solution.py:15
  136.3 1.9 collective-permute-start.6
  138.2 3.1 %collective-permute-done.6 = f32[2,1,7,256]{3,2,0,1:T(8,128)S(1)} collective-permute-done((f32[2,1,7,256]{3,2,0,1:T(8,128)S(1)}, f32[2,1,7,256]{3,2,0,1:T(8,128)S(1)}, u32[]{:S(2)}, u32[]{:S(2)}) %collective-permute-start.6) | collective-permute-done | bytes 14368 | tf_op jit(solution)/shard_map/ppermute | solution.py:18
  142.1 12.5 %all_to_all.56 = f32[32,2,1,512]{3,1,2,0:T(2,128)S(1)} all-to-all(f32[32,2,1,512]{3,1,2,0:T(2,128)S(1)} %constant_dynamic-update-slice_fusion.64), channel_id=1, replica_groups=mesh['tile'=8,'plane'=32] {'plane'}, dimensions={0} | all-to-all | bytes 262144 | tf_op jit(solution)/shard_map/all_to_all | solution.py:63
  155.0 12.5 %all_to_all.57 = f32[2,32,512]{2,0,1:T(2,128)S(1)} all-to-all(f32[2,32,512]{2,0,1:T(2,128)S(1)} %copy.343), channel_id=1, replica_groups=mesh['tile'=8,'plane'=32] {'plane'}, dimensions={1} | all-to-all | bytes 262144 | tf_op jit(solution)/shard_map/all_to_all | solution.py:72
  168.1 13.6 %all_to_all.58 = f32[32,2,1,512]{3,1,2,0:T(2,128)S(1)} all-to-all(f32[32,2,1,512]{3,1,2,0:T(2,128)S(1)} %constant_dynamic-update-slice_fusion.96), channel_id=1, replica_groups=mesh['tile'=8,'plane'=32] {'plane'}, dimensions={0} | all-to-all | bytes 262144 | tf_op jit(solution)/shard_map/all_to_all | solution.py:63
  182.0 12.7 %all_to_all.59 = f32[2,32,512]{2,0,1:T(2,128)S(1)} all-to-all(f32[2,32,512]{2,0,1:T(2,128)S(1)} %copy.346), channel_id=1, replica_groups=mesh['tile'=8,'plane'=32] {'plane'}, dimensions={1} | all-to-all | bytes 262144 | tf_op jit(solution)/shard_map/all_to_all | solution.py:72
  194.8 7.6 %collective-permute-start.7 = (f32[2,1,7,256]{3,2,0,1:T(8,128)S(1)}, f32[2,1,7,256]{3,2,0,1:T(8,128)S(1)}, u32[]{:S(2)}, u32[]{:S(2)}) collective-permute-start(f32[2,1,7,256]{3,2,0,1:T(8,128)S(1)} %get-tuple-element.7), channel_id=1, source_target_pairs={{0,32},{32,64},{64,96},{96,128},{128,160},{160,192},{192,224},{1,3... | collective-permute-start | bytes 43016 | tf_op jit(solution)/shard_map/ppermute | solution.py:15
  202.4 1.9 collective-permute-start.8
  204.5 2.9 %collective-permute-done.8 = f32[2,1,7,256]{3,2,0,1:T(8,128)S(1)} collective-permute-done((f32[2,1,7,256]{3,2,0,1:T(8,128)S(1)}, f32[2,1,7,256]{3,2,0,1:T(8,128)S(1)}, u32[]{:S(2)}, u32[]{:S(2)}) %collective-permute-start.8) | collective-permute-done | bytes 14368 | tf_op jit(solution)/shard_map/ppermute | solution.py:18
  207.8 0.6 fusion.35
  208.7 0.7 multiply_bitcast_fusion
  (181 shorter events, 36.5 us)
Async XLA Ops:
  0.0 9.4 %collective-permute-start = (f32[2,1,32,256]{3,2,0,1:T(8,128)}, f32[2,1,32,256]{3,2,0,1:T(8,128)S(1)}, u32[]{:S(2)}, u32[]{:S(2)}) collective-permute-start(f32[2,1,32,256]{3,2,0,1:T(8,128)} %bitcast.660), channel_id=1, source_target_pairs={{0,32},{32,64},{64,96},{96,128},{128,160},{160,192},{192,224},{1,3... | collective-permute-start | bytes 196616 | tf_op jit(solution)/shard_map/ppermute | solution.py:26
  6.0 3.4 %copy-start = (f32[2,1,64,256]{3,2,1,0:T(8,128)S(1)}, f32[2,1,64,256]{3,2,1,0:T(8,128)}, u32[]{:S(2)}) copy-start(f32[2,1,64,256]{3,2,1,0:T(8,128)} %param.6) | copy-start | bytes 393220
  10.3 4.6 %copy-start.2 = (f32[2,15]{1,0:T(2,128)S(1)}, f32[2,15]{1,0:T(2,128)}, u32[]{:S(2)}) copy-start(f32[2,15]{1,0:T(2,128)} %param.9) | copy-start | bytes 364
  10.5 4.9 %collective-permute-start.1 = (f32[2,1,7,256]{3,2,0,1:T(8,128)S(1)}, f32[2,1,7,256]{3,2,0,1:T(8,128)S(1)}, u32[]{:S(2)}, u32[]{:S(2)}) collective-permute-start(f32[2,1,7,256]{3,2,0,1:T(8,128)S(1)} %get-tuple-element.17), channel_id=1, source_target_pairs={{0,32},{32,64},{64,96},{96,128},{128,160},{160,192},{192,224},{1,3... | collective-permute-start | bytes 43016 | tf_op jit(solution)/shard_map/ppermute | solution.py:15
  12.5 5.1 %collective-permute-start.2 = (f32[2,1,7,256]{3,2,0,1:T(8,128)S(1)}, f32[2,1,7,256]{3,2,0,1:T(8,128)S(1)}, u32[]{:S(2)}, u32[]{:S(2)}) collective-permute-start(f32[2,1,7,256]{3,2,0,1:T(8,128)S(1)} %get-tuple-element.18), channel_id=1, source_target_pairs={{32,0},{64,32},{96,64},{128,96},{160,128},{192,160},{224,192},{33,... | collective-permute-start | bytes 43016 | tf_op jit(solution)/shard_map/ppermute | solution.py:18
  17.8 30.2 %copy-start.1 = (f32[2,41]{1,0:T(2,128)S(1)}, f32[2,41]{1,0:T(2,128)}, u32[]{:S(2)}) copy-start(f32[2,41]{1,0:T(2,128)} %param.8) | copy-start | bytes 988
  36.9 20.8 %all-to-all-start = ((f32[32,2,1,512]{3,1,2,0:T(2,128)}), f32[32,2,1,512]{3,1,2,0:T(2,128)S(1)}, u32[]{:S(2)}, u32[]{:S(2)}) async-start(f32[32,2,1,512]{3,1,2,0:T(2,128)} %constant_dynamic-update-slice_fusion), calls=%async_computation | async-start | bytes 262144 | tf_op jit(solution)/shard_map/all_to_all | solution.py:63
  58.8 13.0 %all-to-all-start.1 = ((f32[2,32,512]{2,0,1:T(2,128)}), f32[2,32,512]{2,0,1:T(2,128)S(1)}, u32[]{:S(2)}, u32[]{:S(2)}) async-start(f32[2,32,512]{2,0,1:T(2,128)} %copy.326), calls=%async_computation.1 | async-start | bytes 262144 | tf_op jit(solution)/shard_map/all_to_all | solution.py:72
  90.9 13.7 %all-to-all-start.2 = ((f32[32,2,1,512]{3,1,2,0:T(2,128)}), f32[32,2,1,512]{3,1,2,0:T(2,128)S(1)}, u32[]{:S(2)}, u32[]{:S(2)}) async-start(f32[32,2,1,512]{3,1,2,0:T(2,128)} %constant_dynamic-update-slice_fusion.32), calls=%async_computation.2 | async-start | bytes 262144 | tf_op jit(solution)/shard_map/all_to_all | solution.py:63
  105.6 13.0 %all-to-all-start.3 = ((f32[2,32,512]{2,0,1:T(2,128)}), f32[2,32,512]{2,0,1:T(2,128)S(1)}, u32[]{:S(2)}, u32[]{:S(2)}) async-start(f32[2,32,512]{2,0,1:T(2,128)} %copy.329), calls=%async_computation.3 | async-start | bytes 262144 | tf_op jit(solution)/shard_map/all_to_all | solution.py:72
  118.7 12.0 %collective-permute-start.3 = (f32[2,1,7,256]{3,2,0,1:T(8,128)S(1)}, f32[2,1,7,256]{3,2,0,1:T(8,128)S(1)}, u32[]{:S(2)}, u32[]{:S(2)}) collective-permute-start(f32[2,1,7,256]{3,2,0,1:T(8,128)S(1)} %get-tuple-element.15), channel_id=1, source_target_pairs={{0,32},{32,64},{64,96},{96,128},{128,160},{160,192},{192,224},{1,3... | collective-permute-start | bytes 43016 | tf_op jit(solution)/shard_map/ppermute | solution.py:15
  125.9 5.1 %collective-permute-start.4 = (f32[2,1,7,256]{3,2,0,1:T(8,128)S(1)}, f32[2,1,7,256]{3,2,0,1:T(8,128)S(1)}, u32[]{:S(2)}, u32[]{:S(2)}) collective-permute-start(f32[2,1,7,256]{3,2,0,1:T(8,128)S(1)} %get-tuple-element.16), channel_id=1, source_target_pairs={{32,0},{64,32},{96,64},{128,96},{160,128},{192,160},{224,192},{33,... | collective-permute-start | bytes 43016 | tf_op jit(solution)/shard_map/ppermute | solution.py:18
  132.9 5.4 %collective-permute-start.5 = (f32[2,1,7,256]{3,2,0,1:T(8,128)S(1)}, f32[2,1,7,256]{3,2,0,1:T(8,128)S(1)}, u32[]{:S(2)}, u32[]{:S(2)}) collective-permute-start(f32[2,1,7,256]{3,2,0,1:T(8,128)S(1)} %get-tuple-element.9), channel_id=1, source_target_pairs={{0,32},{32,64},{64,96},{96,128},{128,160},{160,192},{192,224},{1,3... | collective-permute-start | bytes 43016 | tf_op jit(solution)/shard_map/ppermute | solution.py:15
  136.3 5.1 %collective-permute-start.6 = (f32[2,1,7,256]{3,2,0,1:T(8,128)S(1)}, f32[2,1,7,256]{3,2,0,1:T(8,128)S(1)}, u32[]{:S(2)}, u32[]{:S(2)}) collective-permute-start(f32[2,1,7,256]{3,2,0,1:T(8,128)S(1)} %get-tuple-element.10), channel_id=1, source_target_pairs={{32,0},{64,32},{96,64},{128,96},{160,128},{192,160},{224,192},{33,... | collective-permute-start | bytes 43016 | tf_op jit(solution)/shard_map/ppermute | solution.py:18
  194.8 9.8 %collective-permute-start.7 = (f32[2,1,7,256]{3,2,0,1:T(8,128)S(1)}, f32[2,1,7,256]{3,2,0,1:T(8,128)S(1)}, u32[]{:S(2)}, u32[]{:S(2)}) collective-permute-start(f32[2,1,7,256]{3,2,0,1:T(8,128)S(1)} %get-tuple-element.7), channel_id=1, source_target_pairs={{0,32},{32,64},{64,96},{96,128},{128,160},{160,192},{192,224},{1,3... | collective-permute-start | bytes 43016 | tf_op jit(solution)/shard_map/ppermute | solution.py:15
  202.4 5.1 %collective-permute-start.8 = (f32[2,1,7,256]{3,2,0,1:T(8,128)S(1)}, f32[2,1,7,256]{3,2,0,1:T(8,128)S(1)}, u32[]{:S(2)}, u32[]{:S(2)}) collective-permute-start(f32[2,1,7,256]{3,2,0,1:T(8,128)S(1)} %get-tuple-element.8), channel_id=1, source_target_pairs={{32,0},{64,32},{96,64},{128,96},{160,128},{192,160},{224,192},{33,... | collective-permute-start | bytes 43016 | tf_op jit(solution)/shard_map/ppermute | solution.py:18
